TPU v7x, 32 devices: a whole 2x2x4 slice. The times are simulated.
32 devices in a mesh: row: 8 (over z, y), col: 4 (over x, core).
Axes of the slice: x: 2, y: 2, z: 4, core: 2. Of those that a mesh axis runs over, the one named last changes fastest.
Arguments:
- hidden_act: bfloat16 [768, 26624], P('col', 'row'), may hold values from -6 to 6
- out_grad: bfloat16 [768, 16384], P('row', 'col'), may hold values from -6 to 6
- down_weight: bfloat16 [26624, 16384], P('row', 'col'), may hold values from -0.046875 to 0.046875
Outputs:
- fisher: float32 [26624, 16384], P('row', 'col')
- hidden_grad: bfloat16 [768, 26624], P('col', 'row')
All inputs are finite; a program needn't handle non-finite values.
Results may differ from a plain program's by a relative error of at most 0.001.
Values may be sent and summed in bfloat16 or wider, within the bound.
No kernel may reach another device: no remote copies, remote signals or barrier semaphores. Data moves between devices by JAX's collectives and lax.ppermute only.
A program may use at most 192 MiB of HBM per device.

v0:
```python
import jax
import jax.numpy as jnp
from jax import lax
from jax.sharding import PartitionSpec as P

SEQ = 96
EXAMPLES = 8


def per_device(hidden_act, out_grad, down_weight):
    act_whole = lax.all_gather(hidden_act, "col", axis=0, tiled=True)
    grad_whole = lax.all_gather(out_grad, "row", axis=0, tiled=True)
    feat_rows = down_weight.shape[0]
    feat_cols = down_weight.shape[1]

    def accumulate(example, total):
        start = (example * SEQ).astype(jnp.int32)
        act_piece = lax.dynamic_slice_in_dim(act_whole, start, SEQ, 0)
        grad_piece = lax.dynamic_slice_in_dim(grad_whole, start, SEQ, 0)
        grad_e = lax.dot_general(
            act_piece, grad_piece, (((0,), (0,)), ((), ())), preferred_element_type=jnp.float32
        )
        return total + grad_e * grad_e

    total = lax.fori_loop(0, EXAMPLES, accumulate, jnp.zeros((feat_rows, feat_cols), jnp.float32))
    fisher = total / (EXAMPLES * SEQ)
    summed = lax.psum_scatter(
        lax.dot_general(
            grad_whole, down_weight, (((1,), (1,)), ((), ())), preferred_element_type=jnp.float32
        ),
        "col",
        scatter_dimension=0,
        tiled=True,
    )
    return (fisher, summed.astype(jnp.bfloat16))


def solution(mesh):
    placed = (P("col", "row"), P("row", "col"), P("row", "col"))
    return jax.shard_map(
        per_device,
        mesh=mesh,
        in_specs=placed,
        out_specs=(P("row", "col"), P("col", "row")),
        check_vma=False,
    )
```

profile of v0, /device:TPU:0, one launch (start us, length us, event | category | flops | bytes accessed | tf_op | source)
XLA Modules:
  0.0 478.3 jit_solution(6444310962151930377)
XLA Ops:
  7.2 0.0 all-gather.5.cloned.1.call-start
  7.2 0.7 all-gather.5.cloned.1.call-update
  7.9 0.0 all-gather.3.cloned.1.call-start
  7.9 0.7 all-gather.3.cloned.1.call-update
  8.6 0.0 reduce-scatter.2.cloned.1.call-start
  8.7 102.9 %all-gather.5.cloned.1.call-done = bf16[768,4096]{1,0:T(8,128)(2,1)} async-done(((bf16[96,4096]{1,0:T(8,128)(2,1)}), bf16[768,4096]{1,0:T(8,128)(2,1)}) %all-gather.5.cloned.1.call-update) | async-done | bytes 6291472 | tf_op jit(solution)/shard_map/all_gather | solution.py:12
  111.6 29.3 %fusion.3 = f32[768,3328]{1,0:T(8,128)} fusion(bf16[768,4096]{1,0:T(8,128)(2,1)} %all-gather.5.cloned.1.call-done, bf16[3328,4096]{1,0:T(8,128)(2,1)} %param.7), kind=kOutput, calls=%fused_computation.5 | convolution fusion | flops 20937965568 | bytes 43778048 | tf_op jit(solution)/shard_map/dot_general | solution.py:28
  140.9 0.0 reduce-scatter.2.cloned.1.call-update
  140.9 10.1 %all-gather.3.cloned.1.call-done = bf16[768,3328]{1,0:T(8,128)(2,1)} async-done(((bf16[192,3328]{1,0:T(8,128)(2,1)}), bf16[768,3328]{1,0:T(8,128)(2,1)}) %all-gather.3.cloned.1.call-update) | async-done | bytes 5111824 | tf_op jit(solution)/shard_map/all_gather | solution.py:11
  151.0 282.1 %while.14 = (s32[]{:T(128)}, f32[3328,4096]{1,0:T(8,128)}, bf16[768,3328]{1,0:T(8,128)(2,1)}, bf16[768,4096]{1,0:T(8,128)(2,1)}, s32[]{:T(128)}, /*index=5*/s32[]{:T(128)}, s32[]{:T(128)}, s32[]{:T(128)}) while((s32[]{:T(128)}, f32[3328,4096]{1,0:T(8,128)}, bf16[768,3328]{1,0:T(8,128)(2,1)}, bf16[768,4096]{1,0:T(8,128)(2,1)}, ...), condition=%wide.region_1.0_spmd.clone, body=%wide.region_0.0_spmd.clone.sunk | while | flops 2658140160 | bytes 110478984 | solution.py:25
  151.0 25.6 %select_add_fusion.2 = f32[3328,4096]{1,0:T(8,128)} fusion(f32[3328,4096]{1,0:T(8,128)} %get-tuple-element.139, pred[]{:T(512)S(6)} %compare.3, bf16[768,4096]{1,0:T(8,128)(2,1)} %get-tuple-element.149, s32[]{:T(128)S(6)} %select_n.10, bf16[768,3328]{1,0:T(8,128)(2,1)} %get-tuple-element.148), kind=kOutput, calls=%fused_computation.clone.1 | convolution fusion | flops 2658140160 | bytes 110478848 | tf_op jit(solution)/shard_map/while/body/eval_jaxpr/dot_general | solution.py:20
  176.7 38.3 %select_add_fusion.2 = f32[3328,4096]{1,0:T(8,128)} fusion(f32[3328,4096]{1,0:T(8,128)} %get-tuple-element.139, pred[]{:T(512)S(6)} %compare.3, bf16[768,4096]{1,0:T(8,128)(2,1)} %get-tuple-element.149, s32[]{:T(128)S(6)} %select_n.10, bf16[768,3328]{1,0:T(8,128)(2,1)} %get-tuple-element.148), kind=kOutput, calls=%fused_computation.clone.1 | convolution fusion | flops 2658140160 | bytes 110478848 | tf_op jit(solution)/shard_map/while/body/eval_jaxpr/dot_general | solution.py:20
  215.0 36.6 %select_add_fusion.2 = f32[3328,4096]{1,0:T(8,128)} fusion(f32[3328,4096]{1,0:T(8,128)} %get-tuple-element.139, pred[]{:T(512)S(6)} %compare.3, bf16[768,4096]{1,0:T(8,128)(2,1)} %get-tuple-element.149, s32[]{:T(128)S(6)} %select_n.10, bf16[768,3328]{1,0:T(8,128)(2,1)} %get-tuple-element.148), kind=kOutput, calls=%fused_computation.clone.1 | convolution fusion | flops 2658140160 | bytes 110478848 | tf_op jit(solution)/shard_map/while/body/eval_jaxpr/dot_general | solution.py:20
  251.6 36.3 %select_add_fusion.2 = f32[3328,4096]{1,0:T(8,128)} fusion(f32[3328,4096]{1,0:T(8,128)} %get-tuple-element.139, pred[]{:T(512)S(6)} %compare.3, bf16[768,4096]{1,0:T(8,128)(2,1)} %get-tuple-element.149, s32[]{:T(128)S(6)} %select_n.10, bf16[768,3328]{1,0:T(8,128)(2,1)} %get-tuple-element.148), kind=kOutput, calls=%fused_computation.clone.1 | convolution fusion | flops 2658140160 | bytes 110478848 | tf_op jit(solution)/shard_map/while/body/eval_jaxpr/dot_general | solution.py:20
  287.9 36.3 %select_add_fusion.2 = f32[3328,4096]{1,0:T(8,128)} fusion(f32[3328,4096]{1,0:T(8,128)} %get-tuple-element.139, pred[]{:T(512)S(6)} %compare.3, bf16[768,4096]{1,0:T(8,128)(2,1)} %get-tuple-element.149, s32[]{:T(128)S(6)} %select_n.10, bf16[768,3328]{1,0:T(8,128)(2,1)} %get-tuple-element.148), kind=kOutput, calls=%fused_computation.clone.1 | convolution fusion | flops 2658140160 | bytes 110478848 | tf_op jit(solution)/shard_map/while/body/eval_jaxpr/dot_general | solution.py:20
  324.2 36.3 %select_add_fusion.2 = f32[3328,4096]{1,0:T(8,128)} fusion(f32[3328,4096]{1,0:T(8,128)} %get-tuple-element.139, pred[]{:T(512)S(6)} %compare.3, bf16[768,4096]{1,0:T(8,128)(2,1)} %get-tuple-element.149, s32[]{:T(128)S(6)} %select_n.10, bf16[768,3328]{1,0:T(8,128)(2,1)} %get-tuple-element.148), kind=kOutput, calls=%fused_computation.clone.1 | convolution fusion | flops 2658140160 | bytes 110478848 | tf_op jit(solution)/shard_map/while/body/eval_jaxpr/dot_general | solution.py:20
  360.5 36.3 %select_add_fusion.2 = f32[3328,4096]{1,0:T(8,128)} fusion(f32[3328,4096]{1,0:T(8,128)} %get-tuple-element.139, pred[]{:T(512)S(6)} %compare.3, bf16[768,4096]{1,0:T(8,128)(2,1)} %get-tuple-element.149, s32[]{:T(128)S(6)} %select_n.10, bf16[768,3328]{1,0:T(8,128)(2,1)} %get-tuple-element.148), kind=kOutput, calls=%fused_computation.clone.1 | convolution fusion | flops 2658140160 | bytes 110478848 | tf_op jit(solution)/shard_map/while/body/eval_jaxpr/dot_general | solution.py:20
  396.8 36.3 %select_add_fusion.2 = f32[3328,4096]{1,0:T(8,128)} fusion(f32[3328,4096]{1,0:T(8,128)} %get-tuple-element.139, pred[]{:T(512)S(6)} %compare.3, bf16[768,4096]{1,0:T(8,128)(2,1)} %get-tuple-element.149, s32[]{:T(128)S(6)} %select_n.10, bf16[768,3328]{1,0:T(8,128)(2,1)} %get-tuple-element.148), kind=kOutput, calls=%fused_computation.clone.1 | convolution fusion | flops 2658140160 | bytes 110478848 | tf_op jit(solution)/shard_map/while/body/eval_jaxpr/dot_general | solution.py:20
  433.1 35.8 %broadcast_multiply_fusion = f32[3328,4096]{1,0:T(8,128)} fusion(f32[3328,4096]{1,0:T(8,128)} %get-tuple-element.81), kind=kLoop, calls=%fused_computation.4 | loop fusion | flops 13631488 | bytes 109051904 | tf_op jit(solution)/shard_map/div | solution.py:26
  468.9 0.0 reduce-scatter.2.cloned.1.call-done
  468.9 2.9 convert_element_type.3
  (1 shorter events, 0.0 us)
Async XLA Ops:
  7.2 104.4 %all-gather.5.cloned.1.call-start = ((), (), s32[]{:S(2)}) async-start(), calls=%async_computation.2 | async-start | bytes 7077888 | tf_op jit(solution)/shard_map/all_gather | solution.py:12
  7.9 143.1 %all-gather.3.cloned.1.call-start = ((), (), s32[]{:S(2)}) async-start(), calls=%async_computation.1 | async-start | bytes 6389760 | tf_op jit(solution)/shard_map/all_gather | solution.py:11
  8.6 460.2 %reduce-scatter.2.cloned.1.call-start = ((), (), s32[]{:S(2)}) async-start(), calls=%async_computation.3 | async-start | bytes 12779520 | tf_op jit(solution)/shard_map/reduce_scatter | solution.py:27
Sparse Core Ops, SparseCore 0:
  10.2 101.4 all-gather.4
  113.2 37.8 all-gather.2
  153.7 82.7 reduce-scatter.1
where the time goes:
time: 478 us
  matrix products  311 us (65%)
  waiting for transfers between devices  114 us (24%)
  other arithmetic  38.7 us (8%)
  between operations  13.8 us (3%)
    dot_general x8, matrix products, accumulate(): lax.dot_general(act_piece, grad_piece, (((0,), (0,)), ((), ())), preferre...  282 us
    all_gather x1, waiting for transfers between devices, per_device(): grad_whole = lax.all_gather(out_grad, 'row', axis=0, tiled=True)  103 us
    div x1, other arithmetic, per_device(): fisher = total / (EXAMPLES * SEQ)  35.8 us
    dot_general x1, matrix products, per_device(): lax.dot_general(grad_whole, down_weight, (((1,), (1,)), ((), ())), prefer...  29.3 us
    all_gather x1, waiting for transfers between devices, per_device(): act_whole = lax.all_gather(hidden_act, 'col', axis=0, tiled=True)  10.1 us
  transfers between devices with their start and end apart: 3, of which 2 were waited for; matrix products, arithmetic and copies ran while one was open for 73% of the time, Pallas kernels for 0%

commit v1 on v0

--- a/solution.py
+++ b/solution.py
@@ -9,7 +9,18 @@
 
 def per_device(hidden_act, out_grad, down_weight):
     act_whole = lax.all_gather(hidden_act, "col", axis=0, tiled=True)
-    grad_whole = lax.all_gather(out_grad, "row", axis=0, tiled=True)
+    n_chips = jax.lax.psum(1, "row")
+    buffers = [out_grad]
+    u = 1
+    while u < n_chips:
+        buffers.append(
+            jax.lax.ppermute(
+                buffers[u - 1], "row", [(w, (w - 1) % n_chips) for w in range(n_chips)]
+            )
+        )
+        u = u + 1
+    ready = jnp.concatenate(buffers, axis=0)
+    grad_whole = jnp.roll(ready, jax.lax.axis_index("row") * out_grad.shape[0], axis=0)
     feat_rows = down_weight.shape[0]
     feat_cols = down_weight.shape[1]
 

time: 478 us -> 518 us (1.084)
  starting transfers between devices: 0.11 us -> 37.1 us
  local copies, waits for them, and re-layouts: 0 us -> 25.9 us
  waiting for transfers between devices: 114 us -> 91.3 us
    all_gather x1 -> x0, waiting for transfers between devices: 103 us -> none  [per_device(): grad_whole = lax.all_gather(out_grad, 'row', axis=0, tiled=True)]
    ppermute x0 -> x7, waiting for transfers between devices: none -> 91.2 us  [per_device(): jax.lax.ppermute(buffers[u - 1], 'row', [(w, (w - 1) % n_chips) for w in...]
    ppermute x0 -> x7, starting transfers between devices: none -> 37.1 us  [per_device(): jax.lax.ppermute(buffers[u - 1], 'row', [(w, (w - 1) % n_chips) for w in...]
    unnamed x0 -> x19, local copies, waits for them, and re-layouts: none -> 20.3 us
    all_gather x1, waiting for transfers between devices: 10.1 us -> 0.02 us  [per_device(): act_whole = lax.all_gather(hidden_act, 'col', axis=0, tiled=True)]
  transfers between devices with their start and end apart: 3 -> 9, of which waited for: 2 -> 7; matrix products, arithmetic and copies ran while one was open for 73% -> 71% of each run, Pallas kernels for 0% -> 0%
where the time goes in v1:
time: 518 us
  matrix products  311 us (60%)
  waiting for transfers between devices  91.3 us (18%)
  other arithmetic  38.7 us (7%)
  starting transfers between devices  37.1 us (7%)
  local copies, waits for them, and re-layouts  25.9 us (5%)
  between operations  14.1 us (3%)
    dot_general x8, matrix products, accumulate(): lax.dot_general(act_piece, grad_piece, (((0,), (0,)), ((), ())), preferre...  282 us
    ppermute x7, waiting for transfers between devices, per_device(): jax.lax.ppermute(buffers[u - 1], 'row', [(w, (w - 1) % n_chips) for w in...  91.2 us
    ppermute x7, starting transfers between devices, per_device(): jax.lax.ppermute(buffers[u - 1], 'row', [(w, (w - 1) % n_chips) for w in...  37.1 us
    div x1, other arithmetic, per_device(): fisher = total / (EXAMPLES * SEQ)  35.8 us
    dot_general x1, matrix products, per_device(): lax.dot_general(grad_whole, down_weight, (((1,), (1,)), ((), ())), prefer...  28.6 us
    unnamed x19, local copies, waits for them, and re-layouts  20.3 us
  transfers between devices with their start and end apart: 9, of which 7 were waited for; matrix products, arithmetic and copies ran while one was open for 71% of the time, Pallas kernels for 0%

profile of v1, /device:TPU:0, one launch (start us, length us, event | category | flops | bytes accessed | tf_op | source)
XLA Modules:
  0.0 518.1 jit_solution(691983155803898275)
XLA Ops:
  7.2 0.0 all-gather.2.cloned.1.call-start
  7.2 6.1 %collective-permute-start = (bf16[96,4096]{1,0:T(8,128)(2,1)}, bf16[96,4096]{1,0:T(8,128)(2,1)S(1)}, u32[]{:S(2)}, u32[]{:S(2)}) collective-permute-start(bf16[96,4096]{1,0:T(8,128)(2,1)} %param.6), channel_id=1, source_target_pairs={{0,28},{4,0},{8,4},{12,8},{16,12},{20,16},{24,20},{28,24},{1,29},{... | collective-permute-start | bytes 2359304 | tf_op jit(solution)/shard_map/ppermute | solution.py:17
  13.3 17.1 %collective-permute-done = bf16[96,4096]{1,0:T(8,128)(2,1)S(1)} collective-permute-done((bf16[96,4096]{1,0:T(8,128)(2,1)}, bf16[96,4096]{1,0:T(8,128)(2,1)S(1)}, u32[]{:S(2)}, u32[]{:S(2)}) %collective-permute-start) | collective-permute-done | bytes 786464 | tf_op jit(solution)/shard_map/ppermute | solution.py:17
  30.4 5.1 collective-permute-start.1
  35.5 15.9 %collective-permute-done.1 = bf16[96,4096]{1,0:T(8,128)(2,1)S(1)} collective-permute-done((bf16[96,4096]{1,0:T(8,128)(2,1)S(1)}, bf16[96,4096]{1,0:T(8,128)(2,1)S(1)}, u32[]{:S(2)}, u32[]{:S(2)}) %collective-permute-start.1) | collective-permute-done | bytes 786464 | tf_op jit(solution)/shard_map/ppermute | solution.py:17
  51.4 5.2 collective-permute-start.2
  56.6 15.1 %collective-permute-done.2 = bf16[96,4096]{1,0:T(8,128)(2,1)S(1)} collective-permute-done((bf16[96,4096]{1,0:T(8,128)(2,1)S(1)}, bf16[96,4096]{1,0:T(8,128)(2,1)S(1)}, u32[]{:S(2)}, u32[]{:S(2)}) %collective-permute-start.2) | collective-permute-done | bytes 786464 | tf_op jit(solution)/shard_map/ppermute | solution.py:17
  71.7 5.2 collective-permute-start.3
  76.9 0.0 all-gather.2.cloned.1.call-update
  76.9 0.0 reduce-scatter.2.cloned.1.call-start
  77.0 2.1 constant_dynamic-update-slice_fusion.15
  79.1 12.0 %collective-permute-done.3 = bf16[96,4096]{1,0:T(8,128)(2,1)} collective-permute-done((bf16[96,4096]{1,0:T(8,128)(2,1)S(1)}, bf16[96,4096]{1,0:T(8,128)(2,1)}, u32[]{:S(2)}, u32[]{:S(2)}) %collective-permute-start.3) | collective-permute-done | bytes 786464 | tf_op jit(solution)/shard_map/ppermute | solution.py:17
  91.1 5.3 %collective-permute-start.4 = (bf16[96,4096]{1,0:T(8,128)(2,1)}, bf16[96,4096]{1,0:T(8,128)(2,1)S(1)}, u32[]{:S(2)}, u32[]{:S(2)}) collective-permute-start(bf16[96,4096]{1,0:T(8,128)(2,1)} %collective-permute-done.3), channel_id=1, source_target_pairs={{0,28},{4,0},{8,4},{12,8},{16,12},{20,16},{24,20},{28,24},{1,29},{... | collective-permute-start | bytes 2359304 | tf_op jit(solution)/shard_map/ppermute | solution.py:17
  96.4 1.0 constant_dynamic-update-slice_fusion.14
  97.4 0.9 constant_dynamic-update-slice_fusion.13
  98.3 11.8 %collective-permute-done.4 = bf16[96,4096]{1,0:T(8,128)(2,1)S(1)} collective-permute-done((bf16[96,4096]{1,0:T(8,128)(2,1)}, bf16[96,4096]{1,0:T(8,128)(2,1)S(1)}, u32[]{:S(2)}, u32[]{:S(2)}) %collective-permute-start.4) | collective-permute-done | bytes 786464 | tf_op jit(solution)/shard_map/ppermute | solution.py:17
  110.1 5.1 collective-permute-start.5
  115.2 0.9 constant_dynamic-update-slice_fusion.12
  116.1 2.1 constant_dynamic-update-slice_fusion.11
  118.2 9.5 %collective-permute-done.5 = bf16[96,4096]{1,0:T(8,128)(2,1)S(1)} collective-permute-done((bf16[96,4096]{1,0:T(8,128)(2,1)S(1)}, bf16[96,4096]{1,0:T(8,128)(2,1)S(1)}, u32[]{:S(2)}, u32[]{:S(2)}) %collective-permute-start.5) | collective-permute-done | bytes 786464 | tf_op jit(solution)/shard_map/ppermute | solution.py:17
  127.7 5.2 %collective-permute-start.6 = (bf16[96,4096]{1,0:T(8,128)(2,1)S(1)}, bf16[96,4096]{1,0:T(8,128)(2,1)S(1)}, u32[]{:S(2)}, u32[]{:S(2)}) collective-permute-start(bf16[96,4096]{1,0:T(8,128)(2,1)S(1)} %collective-permute-done.5), channel_id=1, source_target_pairs={{0,28},{4,0},{8,4},{12,8},{16,12},{20,16},{24,20},{28,24},{1,29},{... | collective-permute-start | bytes 2359304 | tf_op jit(solution)/shard_map/ppermute | solution.py:17
  132.9 0.9 constant_dynamic-update-slice_fusion.10
  133.8 1.0 constant_dynamic-update-slice_fusion.9
  134.8 9.8 %collective-permute-done.6 = bf16[96,4096]{1,0:T(8,128)(2,1)S(1)} collective-permute-done((bf16[96,4096]{1,0:T(8,128)(2,1)S(1)}, bf16[96,4096]{1,0:T(8,128)(2,1)S(1)}, u32[]{:S(2)}, u32[]{:S(2)}) %collective-permute-start.6) | collective-permute-done | bytes 786464 | tf_op jit(solution)/shard_map/ppermute | solution.py:17
  144.5 0.9 constant_dynamic-update-slice_fusion.8
  145.5 1.0 constant_dynamic-update-slice_fusion.7
  146.4 0.9 constant_dynamic-update-slice_fusion.6
  147.4 1.0 constant_dynamic-update-slice_fusion.5
  148.4 1.0 constant_dynamic-update-slice_fusion.4
  149.4 2.1 constant_dynamic-update-slice_fusion.3
  151.5 0.9 constant_dynamic-update-slice_fusion.2
  152.5 0.9 constant_dynamic-update-slice_fusion.1
  153.4 1.0 constant_dynamic-update-slice_fusion
  154.3 4.6 constant_dynamic-slice_fusion
  159.0 2.6 copy-done
  161.6 28.6 %fusion.3 = f32[768,3328]{1,0:T(8,128)} fusion(bf16[768,4096]{1,0:T(8,128)(2,1)S(1)} %constant_dynamic-slice_fusion, bf16[3328,4096]{1,0:T(8,128)(2,1)} %param.7), kind=kOutput, calls=%fused_computation.22 | convolution fusion | flops 20937965568 | bytes 43778048 | tf_op jit(solution)/shard_map/dot_general | solution.py:39
  190.2 0.0 all-gather.2.cloned.1.call-done
  190.3 282.4 %while.14 = (s32[]{:T(128)}, f32[3328,4096]{1,0:T(8,128)}, bf16[768,3328]{1,0:T(8,128)(2,1)}, bf16[768,4096]{1,0:T(8,128)(2,1)}, s32[]{:T(128)}, /*index=5*/s32[]{:T(128)}, s32[]{:T(128)}, s32[]{:T(128)}) while((s32[]{:T(128)}, f32[3328,4096]{1,0:T(8,128)}, bf16[768,3328]{1,0:T(8,128)(2,1)}, bf16[768,4096]{1,0:T(8,128)(2,1)}, ...), condition=%wide.region_1.2_spmd.clone, body=%wide.region_0.1_spmd.clone.sunk | while | flops 2658140160 | bytes 110478984 | solution.py:36
  190.3 26.2 %select_add_fusion.2 = f32[3328,4096]{1,0:T(8,128)} fusion(f32[3328,4096]{1,0:T(8,128)} %get-tuple-element.139, pred[]{:T(512)S(6)} %compare.3, bf16[768,4096]{1,0:T(8,128)(2,1)} %get-tuple-element.149, s32[]{:T(128)S(6)} %select_n.25, bf16[768,3328]{1,0:T(8,128)(2,1)} %get-tuple-element.148), kind=kOutput, calls=%fused_computation.clone.1 | convolution fusion | flops 2658140160 | bytes 110478848 | tf_op jit(solution)/shard_map/while/body/eval_jaxpr/dot_general | solution.py:31
  216.4 38.2 %select_add_fusion.2 = f32[3328,4096]{1,0:T(8,128)} fusion(f32[3328,4096]{1,0:T(8,128)} %get-tuple-element.139, pred[]{:T(512)S(6)} %compare.3, bf16[768,4096]{1,0:T(8,128)(2,1)} %get-tuple-element.149, s32[]{:T(128)S(6)} %select_n.25, bf16[768,3328]{1,0:T(8,128)(2,1)} %get-tuple-element.148), kind=kOutput, calls=%fused_computation.clone.1 | convolution fusion | flops 2658140160 | bytes 110478848 | tf_op jit(solution)/shard_map/while/body/eval_jaxpr/dot_general | solution.py:31
  254.6 36.6 %select_add_fusion.2 = f32[3328,4096]{1,0:T(8,128)} fusion(f32[3328,4096]{1,0:T(8,128)} %get-tuple-element.139, pred[]{:T(512)S(6)} %compare.3, bf16[768,4096]{1,0:T(8,128)(2,1)} %get-tuple-element.149, s32[]{:T(128)S(6)} %select_n.25, bf16[768,3328]{1,0:T(8,128)(2,1)} %get-tuple-element.148), kind=kOutput, calls=%fused_computation.clone.1 | convolution fusion | flops 2658140160 | bytes 110478848 | tf_op jit(solution)/shard_map/while/body/eval_jaxpr/dot_general | solution.py:31
  291.2 36.3 %select_add_fusion.2 = f32[3328,4096]{1,0:T(8,128)} fusion(f32[3328,4096]{1,0:T(8,128)} %get-tuple-element.139, pred[]{:T(512)S(6)} %compare.3, bf16[768,4096]{1,0:T(8,128)(2,1)} %get-tuple-element.149, s32[]{:T(128)S(6)} %select_n.25, bf16[768,3328]{1,0:T(8,128)(2,1)} %get-tuple-element.148), kind=kOutput, calls=%fused_computation.clone.1 | convolution fusion | flops 2658140160 | bytes 110478848 | tf_op jit(solution)/shard_map/while/body/eval_jaxpr/dot_general | solution.py:31
  327.5 36.3 %select_add_fusion.2 = f32[3328,4096]{1,0:T(8,128)} fusion(f32[3328,4096]{1,0:T(8,128)} %get-tuple-element.139, pred[]{:T(512)S(6)} %compare.3, bf16[768,4096]{1,0:T(8,128)(2,1)} %get-tuple-element.149, s32[]{:T(128)S(6)} %select_n.25, bf16[768,3328]{1,0:T(8,128)(2,1)} %get-tuple-element.148), kind=kOutput, calls=%fused_computation.clone.1 | convolution fusion | flops 2658140160 | bytes 110478848 | tf_op jit(solution)/shard_map/while/body/eval_jaxpr/dot_general | solution.py:31
  363.8 36.3 %select_add_fusion.2 = f32[3328,4096]{1,0:T(8,128)} fusion(f32[3328,4096]{1,0:T(8,128)} %get-tuple-element.139, pred[]{:T(512)S(6)} %compare.3, bf16[768,4096]{1,0:T(8,128)(2,1)} %get-tuple-element.149, s32[]{:T(128)S(6)} %select_n.25, bf16[768,3328]{1,0:T(8,128)(2,1)} %get-tuple-element.148), kind=kOutput, calls=%fused_computation.clone.1 | convolution fusion | flops 2658140160 | bytes 110478848 | tf_op jit(solution)/shard_map/while/body/eval_jaxpr/dot_general | solution.py:31
  400.1 36.3 %select_add_fusion.2 = f32[3328,4096]{1,0:T(8,128)} fusion(f32[3328,4096]{1,0:T(8,128)} %get-tuple-element.139, pred[]{:T(512)S(6)} %compare.3, bf16[768,4096]{1,0:T(8,128)(2,1)} %get-tuple-element.149, s32[]{:T(128)S(6)} %select_n.25, bf16[768,3328]{1,0:T(8,128)(2,1)} %get-tuple-element.148), kind=kOutput, calls=%fused_computation.clone.1 | convolution fusion | flops 2658140160 | bytes 110478848 | tf_op jit(solution)/shard_map/while/body/eval_jaxpr/dot_general | solution.py:31
  436.4 36.3 %select_add_fusion.2 = f32[3328,4096]{1,0:T(8,128)} fusion(f32[3328,4096]{1,0:T(8,128)} %get-tuple-element.139, pred[]{:T(512)S(6)} %compare.3, bf16[768,4096]{1,0:T(8,128)(2,1)} %get-tuple-element.149, s32[]{:T(128)S(6)} %select_n.25, bf16[768,3328]{1,0:T(8,128)(2,1)} %get-tuple-element.148), kind=kOutput, calls=%fused_computation.clone.1 | convolution fusion | flops 2658140160 | bytes 110478848 | tf_op jit(solution)/shard_map/while/body/eval_jaxpr/dot_general | solution.py:31
  472.7 35.8 %broadcast_multiply_fusion = f32[3328,4096]{1,0:T(8,128)} fusion(f32[3328,4096]{1,0:T(8,128)} %get-tuple-element.81), kind=kLoop, calls=%fused_computation.4 | loop fusion | flops 13631488 | bytes 109051904 | tf_op jit(solution)/shard_map/div | solution.py:37
  508.4 2.9 convert_element_type.3
  (6 shorter events, 0.0 us)
Async XLA Ops:
  7.2 138.3 %copy-start.1 = (bf16[96,4096]{1,0:T(8,128)(2,1)S(1)}, bf16[96,4096]{1,0:T(8,128)(2,1)}, u32[]{:S(2)}) copy-start(bf16[96,4096]{1,0:T(8,128)(2,1)} %param.6) | copy-start | bytes 2359300
  7.2 183.1 %all-gather.2.cloned.1.call-start = ((), (), s32[]{:S(2)}) async-start(), calls=%async_computation.1 | async-start | bytes 6389760 | tf_op jit(solution)/shard_map/all_gather | solution.py:11
  7.2 23.2 %collective-permute-start = (bf16[96,4096]{1,0:T(8,128)(2,1)}, bf16[96,4096]{1,0:T(8,128)(2,1)S(1)}, u32[]{:S(2)}, u32[]{:S(2)}) collective-permute-start(bf16[96,4096]{1,0:T(8,128)(2,1)} %param.6), channel_id=1, source_target_pairs={{0,28},{4,0},{8,4},{12,8},{16,12},{20,16},{24,20},{28,24},{1,29},{... | collective-permute-start | bytes 2359304 | tf_op jit(solution)/shard_map/ppermute | solution.py:17
  30.4 21.0 %collective-permute-start.1 = (bf16[96,4096]{1,0:T(8,128)(2,1)S(1)}, bf16[96,4096]{1,0:T(8,128)(2,1)S(1)}, u32[]{:S(2)}, u32[]{:S(2)}) collective-permute-start(bf16[96,4096]{1,0:T(8,128)(2,1)S(1)} %collective-permute-done), channel_id=1, source_target_pairs={{0,28},{4,0},{8,4},{12,8},{16,12},{20,16},{24,20},{28,24},{1,29},{... | collective-permute-start | bytes 2359304 | tf_op jit(solution)/shard_map/ppermute | solution.py:17
  51.4 20.3 %collective-permute-start.2 = (bf16[96,4096]{1,0:T(8,128)(2,1)S(1)}, bf16[96,4096]{1,0:T(8,128)(2,1)S(1)}, u32[]{:S(2)}, u32[]{:S(2)}) collective-permute-start(bf16[96,4096]{1,0:T(8,128)(2,1)S(1)} %collective-permute-done.1), channel_id=1, source_target_pairs={{0,28},{4,0},{8,4},{12,8},{16,12},{20,16},{24,20},{28,24},{1,29},{... | collective-permute-start | bytes 2359304 | tf_op jit(solution)/shard_map/ppermute | solution.py:17
  71.7 19.4 %collective-permute-start.3 = (bf16[96,4096]{1,0:T(8,128)(2,1)S(1)}, bf16[96,4096]{1,0:T(8,128)(2,1)}, u32[]{:S(2)}, u32[]{:S(2)}) collective-permute-start(bf16[96,4096]{1,0:T(8,128)(2,1)S(1)} %collective-permute-done.2), channel_id=1, source_target_pairs={{0,28},{4,0},{8,4},{12,8},{16,12},{20,16},{24,20},{28,24},{1,29},{... | collective-permute-start | bytes 2359304 | tf_op jit(solution)/shard_map/ppermute | solution.py:17
  76.9 431.5 %reduce-scatter.2.cloned.1.call-start = ((), (), s32[]{:S(2)}) async-start(), calls=%async_computation.2 | async-start | bytes 12779520 | tf_op jit(solution)/shard_map/reduce_scatter | solution.py:38
  91.1 19.0 %collective-permute-start.4 = (bf16[96,4096]{1,0:T(8,128)(2,1)}, bf16[96,4096]{1,0:T(8,128)(2,1)S(1)}, u32[]{:S(2)}, u32[]{:S(2)}) collective-permute-start(bf16[96,4096]{1,0:T(8,128)(2,1)} %collective-permute-done.3), channel_id=1, source_target_pairs={{0,28},{4,0},{8,4},{12,8},{16,12},{20,16},{24,20},{28,24},{1,29},{... | collective-permute-start | bytes 2359304 | tf_op jit(solution)/shard_map/ppermute | solution.py:17
  110.1 17.6 %collective-permute-start.5 = (bf16[96,4096]{1,0:T(8,128)(2,1)S(1)}, bf16[96,4096]{1,0:T(8,128)(2,1)S(1)}, u32[]{:S(2)}, u32[]{:S(2)}) collective-permute-start(bf16[96,4096]{1,0:T(8,128)(2,1)S(1)} %collective-permute-done.4), channel_id=1, source_target_pairs={{0,28},{4,0},{8,4},{12,8},{16,12},{20,16},{24,20},{28,24},{1,29},{... | collective-permute-start | bytes 2359304 | tf_op jit(solution)/shard_map/ppermute | solution.py:17
  127.7 16.9 %collective-permute-start.6 = (bf16[96,4096]{1,0:T(8,128)(2,1)S(1)}, bf16[96,4096]{1,0:T(8,128)(2,1)S(1)}, u32[]{:S(2)}, u32[]{:S(2)}) collective-permute-start(bf16[96,4096]{1,0:T(8,128)(2,1)S(1)} %collective-permute-done.5), channel_id=1, source_target_pairs={{0,28},{4,0},{8,4},{12,8},{16,12},{20,16},{24,20},{28,24},{1,29},{... | collective-permute-start | bytes 2359304 | tf_op jit(solution)/shard_map/ppermute | solution.py:17
  159.0 2.6 copy-start
Sparse Core Ops, SparseCore 0:
  77.0 36.9 all-gather.1
  190.4 84.5 reduce-scatter.1
